TPU v7x, 128 devices: a whole 4x4x4 slice. The times are simulated.
128 devices in a mesh: sec: 2 (over core), dev: 64 (over z, x, y).
Axes of the slice: x: 4, y: 4, z: 4, core: 2. Of those that a mesh axis runs over, the one named last changes fastest.
Arguments:
- queries: bfloat16 [256, 4, 6144], P('dev'), may hold values from -160 to 160
- cache_keys: bfloat16 [256, 128, 1024], P('dev'), may hold values from -8 to 8
- cache_values: bfloat16 [256, 128, 1024], P('dev'), may hold values from -6 to 6
- lengths: int32 [256], P('dev'), may hold values from 1 to 128, 16384 in all
- new_keys: bfloat16 [256, 4, 1024], P('dev'), may hold values from -6 to 6
- new_values: bfloat16 [256, 4, 1024], P('dev'), may hold values from -6 to 6
- residual: bfloat16 [256, 4, 6144], P('dev'), may hold values from -6 to 6
- norm_gain: float32 [6144], replicated, may hold values from 0.25 to 1.75
- expert_ids: int32 [1024, 2], P('dev'), may hold values from 0 to 3, all different within a row; in each aligned block of 16 rows (0 to 15, 16 to 31, ...) at most 9 rows name the same one
- gate_logits: float32 [1024, 2], P('dev'), may hold values from -8 to 8
- w_gate: bfloat16 [6144, 32768], P(None, 'dev'), may hold values from -0.078125 to 0.078125
- w_up: bfloat16 [6144, 32768], P(None, 'dev'), may hold values from -0.078125 to 0.078125
- w_down: bfloat16 [32768, 6144], P('dev'), may hold values from -0.0625 to 0.0625
Outputs:
- layer_out: bfloat16 [256, 4, 6144], P('dev', None, 'sec')
Inputs may be any that keep to these rules, and one draw needn't show every extreme that they name: `expert_ids`: in the 16 tokens of one attention device no expert is named more than 9 times; some expert is named exactly 9 times in some of these blocks.
All inputs are finite; a program needn't handle non-finite values. No bound on the sum of `lengths` on one device may be relied on, other than what follows from the above.
Results may differ from a plain program's by a relative error of at most 0.0065.
Values may be sent and summed in bfloat16 or wider, within the bound.
A program may use at most 192 MiB of HBM per device.

v0:
```python
import jax
import jax.numpy as jnp
from jax import lax
from jax.sharding import PartitionSpec as P

HEADS = 48
KVH = 8
HD = 128
EXP = 4
LMAX = 128
CAP = 9


epsilon = 1e-05


def from_behind(x, axis, by):
    size = lax.axis_size(axis)
    pairs = [(i, i + by) for i in range(size) if 0 <= i + by < size]
    return lax.ppermute(x, axis, pairs)


def attend_local(operands):
    queries, cache_keys, cache_values, lengths, new_keys, new_values, residual, norm_gain = operands
    requests = queries.shape[0]
    steps = queries.shape[1]
    width = residual.shape[2]
    per_group = HEADS // KVH
    key_all = jnp.concatenate([cache_keys, new_keys], axis=1).reshape(
        requests, LMAX + steps, KVH, HD
    )
    value_all = jnp.concatenate([cache_values, new_values], axis=1).reshape(
        requests, LMAX + steps, KVH, HD
    )
    query_heads = queries.reshape(requests, steps, KVH, per_group, HD)
    scores = jnp.einsum(
        "rsgqd,rlgd->rsgql", query_heads, key_all, preferred_element_type=jnp.float32
    ) * HD ** (-0.5)
    position = jnp.arange(LMAX + steps, dtype=jnp.int32)
    stepnum = jnp.arange(steps, dtype=jnp.int32)
    in_cache = position[None, None, :] < lengths[:, None, None]
    in_window = (position[None, :] >= LMAX) & (position[None, :] - LMAX <= stepnum[:, None])
    valid = in_cache | in_window[None, :, :]
    scores = jnp.where(valid[:, :, None, None, :], scores, jnp.float32(-1e30))
    peak = jnp.max(scores, axis=-1, keepdims=True)
    expo = jnp.exp(scores - peak)
    probs = (expo / jnp.sum(expo, axis=-1, keepdims=True)).astype(jnp.bfloat16)
    attended = jnp.einsum("rsgql,rlgd->rsgqd", probs, value_all, preferred_element_type=jnp.float32)
    attended = attended.reshape(requests, steps, width)
    hstate = (residual.astype(jnp.float32) + attended).astype(jnp.bfloat16)
    hfloat = hstate.astype(jnp.float32)
    meansq = jnp.mean(hfloat * hfloat, axis=-1, keepdims=True)
    normed = (hfloat * lax.rsqrt(meansq + epsilon) * norm_gain).astype(jnp.bfloat16)
    return (hstate, normed)


def attend_skip(operands):
    residual = operands[6]
    return (jnp.zeros_like(residual), jnp.zeros_like(residual))


def expert_rows(rows, w_gate, w_up, w_down):
    gate = jnp.dot(rows, w_gate, preferred_element_type=jnp.float32)
    upward = jnp.dot(rows, w_up, preferred_element_type=jnp.float32)
    hidden = (jax.nn.silu(gate) * upward).astype(jnp.bfloat16)
    return jnp.dot(hidden, w_down, preferred_element_type=jnp.float32).astype(jnp.bfloat16)


def shards(
    queries,
    cache_keys,
    cache_values,
    lengths,
    new_keys,
    new_values,
    residual,
    norm_gain,
    expert_ids,
    gate_logits,
    w_gate,
    w_up,
    w_down,
):
    is_attention = lax.axis_index("sec") == 0
    is_expert = jnp.logical_not(is_attention)
    devices = lax.axis_size("dev")
    group = devices // EXP
    my_expert = lax.axis_index("dev") // group
    requests = residual.shape[0]
    steps = residual.shape[1]
    width = residual.shape[2]
    half = width // 2
    tok_rows = requests * steps
    operands = (
        queries,
        cache_keys,
        cache_values,
        lengths,
        new_keys,
        new_values,
        residual,
        norm_gain,
    )
    hstate, normed = lax.cond(is_attention, attend_local, attend_skip, operands)
    flat_h = hstate.reshape(tok_rows, width)
    flat_in = normed.reshape(tok_rows, width)
    flat_ids = expert_ids.reshape(-1)
    onehot = (flat_ids[:, None] == jnp.arange(EXP, dtype=jnp.int32)[None, :]).astype(jnp.int32)
    ranks = jnp.cumsum(onehot, axis=0) - onehot
    slot_of = jnp.sum(ranks * onehot, axis=1)
    target = (flat_ids * CAP + slot_of).reshape(tok_rows, 2)
    slot_rows = jnp.arange(EXP * CAP, dtype=jnp.int32)
    first_hit = target[:, 0:1] == slot_rows[None, :]
    second_hit = target[:, 1:2] == slot_rows[None, :]
    placing = jnp.logical_or(first_hit, second_hit).astype(jnp.bfloat16)
    buffer = lax.dot_general(
        placing, flat_in, (((0,), (0,)), ((), ())), preferred_element_type=jnp.float32
    )
    buffer = buffer.astype(jnp.bfloat16).reshape(EXP, CAP, width)
    weights = jax.nn.softmax(gate_logits, axis=-1)
    mixing = weights[:, 0:1] * first_hit.astype(jnp.float32) + weights[:, 1:2] * second_hit.astype(
        jnp.float32
    )
    moved_rows, moved_high = from_behind((buffer, flat_h[:, half:]), "sec", 1)
    mine = lax.dynamic_index_in_dim(
        lax.all_gather(moved_rows, "dev", axis=1, tiled=True), my_expert, 0, keepdims=False
    )
    partials = lax.cond(
        is_expert,
        lambda block: expert_rows(block, w_gate, w_up, w_down),
        lambda block: jnp.zeros_like(block),
        mine,
    )
    partials = partials.reshape(devices, CAP, width)
    returned = lax.all_to_all(partials, "dev", split_axis=0, concat_axis=0, tiled=True)
    summed = jnp.sum(returned.reshape(EXP, group, CAP, width).astype(jnp.float32), axis=1)
    mixed = jnp.dot(
        mixing,
        summed.reshape(EXP * CAP, width),
        precision=lax.Precision.HIGHEST,
        preferred_element_type=jnp.float32,
    )
    upper_out = (moved_high.astype(jnp.float32) + mixed[:, half:]).astype(jnp.bfloat16)
    lower_mix = from_behind(mixed[:, :half], "sec", -1)
    lower_out = (flat_h[:, :half].astype(jnp.float32) + lower_mix).astype(jnp.bfloat16)
    layer_out = jnp.where(is_attention, lower_out, upper_out)
    return layer_out.reshape(requests, steps, half)


def solution(mesh):
    return jax.shard_map(
        shards,
        mesh=mesh,
        in_specs=(
            P("dev", None, None),
            P("dev", None, None),
            P("dev", None, None),
            P("dev"),
            P("dev", None, None),
            P("dev", None, None),
            P("dev", None, None),
            P(),
            P("dev", None),
            P("dev", None),
            P(None, "dev"),
            P(None, "dev"),
            P("dev", None),
        ),
        out_specs=P("dev", None, "sec"),
        check_vma=False,
    )
```

profile of v0, /device:TPU:32, one launch (start us, length us, event | category | flops | bytes accessed | tf_op | source)
XLA Modules:
  0.0 400.5 jit_solution(4926750830387768052)
XLA Ops:
  6.5 0.0 all-gather.2.cloned.1.call-start
  6.5 0.8 copy.52
  7.3 0.1 eq.49
  7.4 0.1 fusion.29
  7.5 0.1 reduce_window_sum.11
  7.5 0.2 select_reduce_fusion
  7.7 0.1 reduce_sum.48
  7.8 0.1 copy.53
  7.9 0.7 multiply_add_fusion
  8.6 10.0 %conditional.2 = (bf16[4,4,6144]{2,1,0:T(4,128)(2,1)}, bf16[16,6144]{1,0:T(8,128)(2,1)S(1)}) conditional(s32[]{:T(128)} %convert_element_type.60, () %tuple.36, (bf16[4,4,6144]{2,1,0:T(4,128)(2,1)}, bf16[4,128,1024]{2,1,0:T(8,128)(2,1)}, bf16[4,4,1024]{2,1,0:T(4,128)(2,1)}, s32[4]{0:T(128)}, bf16[4,128,1024]{2,1,0:T(8,128)(2,1)}, ...), branch_computations={%region_0.1_spmd, %region_1.5_spmd} | conditional | flops 57825292 | bytes 17463132 | solution.py:104
  8.6 0.7 iota_compare_fusion.1
  9.3 0.0 copy-start.1
  9.3 1.9 pad_maximum_fusion
  11.3 0.6 reshape.112
  11.8 0.0 copy-done.1
  11.9 0.2 reshape.113
  12.1 1.9 fusion.46
  14.0 0.6 reshape.111
  14.6 0.0 copy-start.2
  14.6 1.7 convolution_bitcast_fusion
  16.3 0.0 copy-start.3
  16.4 0.2 reshape.114
  16.6 0.0 copy-done.2
  16.6 0.9 fusion.8
  17.5 1.1 fusion.10
  18.6 0.4 convolution_convert_fusion.1
  19.0 0.2 reshape.122
  19.2 0.4 copy.54
  19.6 1.3 collective-permute-start
  20.9 1.4 collective-permute-done
  22.3 0.8 copy-done
  23.0 0.0 all-gather.2.cloned.1.call-update
  23.1 144.5 %all-gather.2.cloned.1.call-done = bf16[4,576,6144]{2,0,1:T(4,128)(2,1)} async-done(((bf16[4,9,6144]{2,0,1:T(4,128)(2,1)}), bf16[4,576,6144]{2,0,1:T(4,128)(2,1)}) %all-gather.2.cloned.1.call-update) | async-done | bytes 28311568 | tf_op jit(solution)/shard_map/all_gather | solution.py:126
  167.5 3.7 conditional.3
  167.5 3.7 broadcast.108
  171.3 10.2 %reshape.123 = bf16[64,9,6144]{2,1,0:T(8,128)(2,1)} reshape(bf16[576,6144]{1,0:T(8,128)(2,1)} %get-tuple-element.235) | data formatting | bytes 14155776 | tf_op jit(solution)/shard_map/reshape | solution.py:134
  181.5 9.1 %all-to-all-start = ((bf16[64,9,6144]{2,1,0:T(8,128)(2,1)}), bf16[64,9,6144]{2,1,0:T(8,128)(2,1)}, u32[]{:S(2)}, u32[]{:S(2)}) async-start(bf16[64,9,6144]{2,1,0:T(8,128)(2,1)} %reshape.123), calls=%async_computation | async-start | bytes 25165824 | tf_op jit(solution)/shard_map/all_to_all | solution.py:135
  190.6 0.0 copy-done.4
  190.7 165.3 %all-to-all-done = bf16[64,9,6144]{2,1,0:T(8,128)(2,1)} async-done(((bf16[64,9,6144]{2,1,0:T(8,128)(2,1)}), bf16[64,9,6144]{2,1,0:T(8,128)(2,1)}, u32[]{:S(2)}, u32[]{:S(2)}) %all-to-all-start) | async-done | bytes 7077920 | tf_op jit(solution)/shard_map/all_to_all | solution.py:135
  356.0 6.8 %convert_reduce_fusion = f32[4,9,6144]{2,1,0:T(8,128)S(1)} fusion(bf16[64,9,6144]{2,1,0:T(8,128)(2,1)} %all-to-all-done), kind=kLoop, calls=%fused_computation.38 | loop fusion | flops 6856704 | bytes 7962624 | tf_op jit(solution)/shard_map/reduce_sum | solution.py:136
  362.9 0.1 reshape.124
  363.0 0.7 fusion.30
  363.7 1.3 collective-permute-start.1
  365.0 1.0 reshape.121
  366.0 26.0 %collective-permute-start.2 = (bf16[16,3072]{1,0:T(8,128)(2,1)S(1)}, bf16[16,3072]{1,0:T(8,128)(2,1)S(1)}, u32[]{:S(2)}, u32[]{:S(2)}) collective-permute-start(bf16[16,3072]{1,0:T(8,128)(2,1)S(1)} %slice.34), channel_id=1, source_target_pairs={{0,64},{1,65},{2,66},{3,67},{4,68},{5,69},{6,70},{7,71},{8,72},{9,... | collective-permute-start | bytes 294920 | tf_op jit(solution)/shard_map/ppermute | solution.py:20
  392.0 0.9 collective-permute-done.2
  392.9 0.0 collective-permute-done.1
  393.0 0.7 reshape.125
  (17 shorter events, 0.3 us)
Async XLA Ops:
  6.5 161.0 %all-gather.2.cloned.1.call-start = ((), (), s32[]{:S(2)}) async-start(), calls=%async_computation.1 | async-start | bytes 28753920 | tf_op jit(solution)/shard_map/all_gather | solution.py:126
  9.3 2.5 copy-start.1
  14.6 2.0 copy-start.2
  16.3 1.2 copy-start.3
  19.6 2.7 collective-permute-start
  22.3 0.8 copy-start
  181.5 9.2 %copy-start.4 = (f32[16,2]{0,1:T(2,128)S(1)}, f32[16,2]{0,1:T(2,128)}, u32[]{:S(2)}) copy-start(f32[16,2]{0,1:T(2,128)} %param.26) | copy-start | bytes 388
  181.5 174.5 %all-to-all-start = ((bf16[64,9,6144]{2,1,0:T(8,128)(2,1)}), bf16[64,9,6144]{2,1,0:T(8,128)(2,1)}, u32[]{:S(2)}, u32[]{:S(2)}) async-start(bf16[64,9,6144]{2,1,0:T(8,128)(2,1)} %reshape.123), calls=%async_computation | async-start | bytes 25165824 | tf_op jit(solution)/shard_map/all_to_all | solution.py:135
  363.7 29.2 %collective-permute-start.1 = (f32[16,3072]{1,0:T(8,128)S(1)}, f32[16,3072]{1,0:T(8,128)S(1)}, u32[]{:S(2)}, u32[]{:S(2)}) collective-permute-start(f32[16,3072]{1,0:T(8,128)S(1)} %slice.33), channel_id=1, source_target_pairs={{64,0},{65,1},{66,2},{67,3},{68,4},{69,5},{70,6},{71,7},{72,8},{73... | collective-permute-start | bytes 589832 | tf_op jit(solution)/shard_map/ppermute | solution.py:20
  366.0 26.9 %collective-permute-start.2 = (bf16[16,3072]{1,0:T(8,128)(2,1)S(1)}, bf16[16,3072]{1,0:T(8,128)(2,1)S(1)}, u32[]{:S(2)}, u32[]{:S(2)}) collective-permute-start(bf16[16,3072]{1,0:T(8,128)(2,1)S(1)} %slice.34), channel_id=1, source_target_pairs={{0,64},{1,65},{2,66},{3,67},{4,68},{5,69},{6,70},{7,71},{8,72},{9,... | collective-permute-start | bytes 294920 | tf_op jit(solution)/shard_map/ppermute | solution.py:20
Sparse Core Ops, SparseCore 0:
  23.2 144.2 all-gather.1
where the time goes:
time: 404 us; the launch traced here: 401 us
  waiting for transfers between devices  312 us (77%)
  starting transfers between devices  37.8 us (9%)
  local copies, waits for them, and re-layouts  19.7 us (5%)
  between operations  13.5 us (3%)
  other arithmetic  12.6 us (3%)
  matrix products  4.7 us (1%)
    all_to_all x1, waiting for transfers between devices, shards(): lax.all_to_all(partials, 'dev', split_axis=0, concat_axis=0, tiled=True)  165 us
    all_gather x1, waiting for transfers between devices, shards(): lax.all_gather(moved_rows, 'dev', axis=1, tiled=True)  144 us
    ppermute x3, starting transfers between devices, from_behind(): return lax.ppermute(x, axis, pairs)  28.6 us
    reshape x1, local copies, waits for them, and re-layouts, shards(): partials = partials.reshape(devices, CAP, width)  10.2 us
    all_to_all x1, starting transfers between devices, shards(): lax.all_to_all(partials, 'dev', split_axis=0, concat_axis=0, tiled=True)  9.15 us
  transfers between devices with their start and end apart: 5, of which 4 were waited for; matrix products, arithmetic and copies ran while one was open for 0% of the time, Pallas kernels for 0%

commit v1 on v0

v1 whole, which is shorter than its diff:
```python
import functools

import jax
import jax.numpy as jnp
from jax import lax
from jax.experimental import pallas as pl
from jax.experimental.pallas import tpu as pltpu
from jax.sharding import PartitionSpec as P

HEADS = 48
KVH = 8
HD = 128
EXP = 4
LMAX = 128
CAP = 9
SIDE = 4
EPS = 1e-05

F32 = jnp.float32
BF16 = jnp.bfloat16
HALF = 3072
FF = 512
FA = 1408
FB = HALF - FA
NSEM = 200
TILE = 256
GROUPS = (
    ((0, 0), (1, 0), (-1, 0), (0, 1), (0, -1)),
    ((1, 1), (1, -1), (-1, 1), (-1, -1), (2, 0), (0, 2)),
    ((2, 1), (2, -1), (1, 2), (-1, 2), (2, 2)),
)


def lanes(j, n=128):
    return slice(j * n, (j + 1) * n)


def kernel(
    lens, q_hbm, k_hbm, v_hbm, nk_hbm, nv_hbm, res_hbm, gain, ids, logits, wg_hbm, wu_hbm, wd_hbm,
    out,
    qb, kb, vb, nkb, nvb, resb, hb, xn, ssb, ssr,
    zs, zr, zos, zor, X, XOs, XO, W, Wd, GU, GUs, GUr, H, Pb, PO, PS,
    ad, af, ad2, af2, bd, bf, bd2, bf2, od, of, od2, of2, rzs, rzr, rzos, rzor,
    lsem, ssem, rsem,
):
    c = lax.axis_index("sec")
    d = lax.axis_index("dev")
    z = d // 16
    x = (d // 4) % 4
    y = d % 4
    here = x * 4 + y

    def near(v, by):
        return lax.rem(v + (by % 4), 4)

    def chip(dz=0, dx=0, dy=0):
        return near(z, dz) * 16 + near(x, dx) * 4 + near(y, dy)

    steps = {"x": lambda by: (c, chip(dx=by)), "y": lambda by: (c, chip(dy=by))}
    zpeers = [(c, chip(dz=k)) for k in (1, 2, 3)]
    sibling = (1 - c, d)
    partners = zpeers + [sibling] + [steps[a](by) for a in ("x", "y") for by in (1, -1)]

    barrier = pltpu.get_barrier_semaphore()
    for p in partners:
        pl.semaphore_signal(barrier, inc=1, device_id=p, device_id_type=pl.DeviceIdType.MESH)

    feats = pl.ds(pl.multiple_of(c * HALF, HALF), HALF)
    kvs = pl.ds(pl.multiple_of(c * 512, 512), 512)
    local = []
    for i, (src, dst) in enumerate((
        (q_hbm.at[:, :, feats], qb),
        (k_hbm.at[:, :, kvs], kb),
        (nk_hbm.at[:, :, kvs], nkb),
        (v_hbm.at[:, :, kvs], vb),
        (nv_hbm.at[:, :, kvs], nvb),
        (res_hbm.at[:, :, feats], resb),
        (wg_hbm.at[feats, :], W.at[:, pl.ds(0, FF)]),
        (wu_hbm.at[feats, :], W.at[:, pl.ds(FF, FF)]),
        (wd_hbm.at[:, feats], Wd),
    )):
        copy = pltpu.make_async_copy(src, dst, lsem.at[i])
        copy.start()
        local.append(copy)

    counter = [0]
    sent = []

    def new_id():
        counter[0] += 1
        return counter[0] - 1

    def send(src, dst, sem, dev):
        copy = pltpu.make_async_remote_copy(
            src_ref=src, dst_ref=dst, send_sem=ssem.at[sem], recv_sem=rsem.at[sem],
            device_id=dev, device_id_type=pl.DeviceIdType.MESH,
        )
        copy.start()
        sent.append(copy)

    def take(dst, sem, dev):
        pltpu.make_async_remote_copy(
            src_ref=dst, dst_ref=dst, send_sem=ssem.at[sem], recv_sem=rsem.at[sem],
            device_id=dev, device_id_type=pl.DeviceIdType.MESH,
        ).wait_recv()

    for copy in local[:6]:
        copy.wait()
    row = lax.broadcasted_iota(jnp.int32, (96, 128), 0)
    col = lax.broadcasted_iota(jnp.int32, (96, 128), 1)
    lenv = jnp.concatenate([jnp.full((24, 128), lens[r], jnp.int32) for r in range(4)], axis=0)
    in_cache = col < lenv
    row16 = lax.broadcasted_iota(jnp.int32, (96, 16), 0)
    col16 = lax.broadcasted_iota(jnp.int32, (96, 16), 1)
    in_window = (row16 // 24 == col16 // 4) & (col16 % 4 <= row16 % 4)
    scale = HD ** (-0.5)
    ss = jnp.zeros((16, 128), F32)
    contract = (((1,), (1,)), ((), ()))
    for g in range(4):
        qs = [
            jnp.concatenate([qb[r, :, lanes(g * 6 + h)].astype(F32) for h in range(6)], axis=0)
            for r in range(4)
        ]
        sc = jnp.concatenate([
            lax.dot_general(qs[r].astype(BF16), kb[r, :, lanes(g)], contract, preferred_element_type=F32)
            for r in range(4)
        ], axis=0) * scale
        nk = jnp.concatenate([nkb[r, :, lanes(g)].astype(F32) for r in range(4)], axis=0).astype(BF16)
        nv = jnp.concatenate([nvb[r, :, lanes(g)].astype(F32) for r in range(4)], axis=0).astype(BF16)
        qa = jnp.concatenate(qs, axis=0).astype(BF16)
        sn = lax.dot_general(qa, nk, contract, preferred_element_type=F32) * scale
        sc = jnp.where(in_cache, sc, -1e30)
        sn = jnp.where(in_window, sn, -1e30)
        peak = jnp.maximum(jnp.max(sc, axis=1, keepdims=True), jnp.max(sn, axis=1, keepdims=True))
        ec = jnp.exp(sc - peak)
        en = jnp.exp(sn - peak)
        total = jnp.sum(ec, axis=1, keepdims=True) + jnp.sum(en, axis=1, keepdims=True)
        inv = 1.0 / total
        pc = ec * inv
        pn = (en * inv).astype(BF16)
        att = jnp.concatenate([
            jnp.dot(pc[24 * r:24 * r + 24].astype(BF16), vb[r, :, lanes(g)], preferred_element_type=F32)
            for r in range(4)
        ], axis=0) + jnp.dot(pn, nv, preferred_element_type=F32)
        for h in range(6):
            j = g * 6 + h
            part = jnp.concatenate([att[r * 24 + h * 4:r * 24 + h * 4 + 4] for r in range(4)], axis=0)
            res = jnp.concatenate([resb[r, :, lanes(j)].astype(F32) for r in range(4)], axis=0)
            hst = (res + part).astype(BF16)
            hb[:, lanes(j)] = hst
            hf = hst.astype(F32)
            ss = ss + hf * hf
    ssb[...] = jnp.broadcast_to(jnp.sum(ss, axis=1, keepdims=True), (16, 128))
    pl.semaphore_wait(barrier, len(partners))
    sid = new_id()
    send(ssb, ssr, sid, sibling)

    idv = ids[...]
    id0, id1 = idv[:, 0:1], idv[:, 1:2]
    slot = lax.broadcasted_iota(jnp.int32, (16, 128), 1)
    who = jnp.where(slot < 32, slot // 8, slot - 32)
    rank = jnp.where(slot < 32, slot % 8, 8)
    hit0 = id0 == who
    hit1 = id1 == who
    hit = jnp.where(hit0 | hit1, 1.0, 0.0)
    before = jnp.where(
        lax.broadcasted_iota(jnp.int32, (16, 16), 1) < lax.broadcasted_iota(jnp.int32, (16, 16), 0), 1.0, 0.0
    )
    ahead = jnp.dot(before.astype(BF16), hit.astype(BF16), preferred_element_type=F32)
    chosen = ahead == rank.astype(F32)
    pick0 = jnp.where(hit0 & chosen, 1.0, 0.0)
    pick1 = jnp.where(hit1 & chosen, 1.0, 0.0)
    packing = jnp.transpose(pick0 + pick1)[0:48].astype(BF16)
    lg = logits[...]
    l0, l1 = lg[:, 0:1], lg[:, 1:2]
    top = jnp.maximum(l0, l1)
    e0, e1 = jnp.exp(l0 - top), jnp.exp(l1 - top)
    w0 = e0 / (e0 + e1)
    w1 = e1 / (e0 + e1)

    take(ssr, sid, sibling)
    inv = lax.rsqrt((ssb[...] + ssr[...]) / (2 * HALF) + EPS)
    gains = gain[pl.ds(pl.multiple_of(c * 24, 8), 24), :]
    for j in range(24):
        xn[:, lanes(j)] = (hb[:, lanes(j)].astype(F32) * inv * gains[j:j + 1]).astype(BF16)
    for n in range(4):
        at = lanes(n, 768)
        packed = jnp.dot(packing, xn[:, at], preferred_element_type=F32)
        for e in range(4):
            zs[e, :, at] = packed[8 * e:8 * e + 8].astype(BF16)
            zos[e, :, at] = packed[32 + e:33 + e]

    zid = [(new_id(), new_id()) for _ in range(3)]
    for k in (1, 3, 2):
        e = near(z, k)
        send(zs.at[e], zr.at[z], zid[k - 1][0], (c, chip(dz=k)))
        send(zos.at[e], zor.at[z], zid[k - 1][1], (c, chip(dz=k)))
    zr[z] = zs[z]
    zor[z] = zos[z]
    for k in (1, 3, 2):
        frm = near(z, -k)
        take(zr.at[frm], zid[k - 1][0], (c, chip(dz=k)))
        take(zor.at[frm], zid[k - 1][1], (c, chip(dz=k)))
    for n in range(4):
        at = lanes(n, 768)
        X[here, :, at] = jnp.concatenate([zr[s, :, at].astype(F32) for s in range(4)], axis=0).astype(BF16)
    for s in range(4):
        XOs[y, s:s + 1, :] = zor[s]

    def blk(dx, dy):
        return near(x, dx) * 4 + near(y, dy)

    class Gather:
        def __init__(self, axis, view, size, cut):
            self.view, self.size, self.cut = view, size, cut
            self.dev = {by: steps[axis](by) for by in (1, -1)}
            self.op, self.om, self.fp, self.fm = new_id(), new_id(), new_id(), new_id()

        def start(self):
            v = self.view(0, 0, self.size)
            send(v, v, self.op, self.dev[1])
            send(v, v, self.om, self.dev[-1])

        def near(self):
            take(self.view(-1, 0, self.size), self.op, self.dev[1])
            v = self.view(-1, 0, self.cut)
            send(v, v, self.fp, self.dev[1])
            take(self.view(1, 0, self.size), self.om, self.dev[-1])
            v = self.view(1, self.cut, self.size - self.cut)
            send(v, v, self.fm, self.dev[-1])

        def far(self):
            take(self.view(2, 0, self.cut), self.fp, self.dev[1])
            take(self.view(2, self.cut, self.size - self.cut), self.fm, self.dev[-1])

    order = (0, 1, -1, 2)
    cut_a = {0: 640, 1: 768, -1: 640, 2: 768}
    cut_b = {0: 768, 1: 896, -1: 768, 2: 896}
    a1 = Gather("y", lambda r, lo, n: X.at[blk(0, r), :, pl.ds(lo, n)], FA, 640)
    b1 = Gather("x", lambda r, lo, n: X.at[blk(r, 0), :, pl.ds(FA + lo, n)], FB, 896)
    o1 = Gather("y", lambda r, lo, n: XOs.at[near(y, r), :, pl.ds(lo, n)], HALF, 1536)
    a2 = {
        k: Gather("x", lambda r, lo, n, k=k: X.at[blk(r, k), :, pl.ds(lo, n)], FA, cut_a[k]) for k in order
    }
    b2 = {
        k: Gather("y", lambda r, lo, n, k=k: X.at[blk(k, r), :, pl.ds(FA + lo, n)], FB, cut_b[k]) for k in order
    }
    o2 = Gather("x", lambda r, lo, n: XO.at[near(x, r), :, pl.ds(lo, n)], HALF, 1536)

    a1.start()
    b1.start()
    o1.start()
    a2[0].start()
    b2[0].start()

    a1.near()
    b1.near()
    for k in (1, -1):
        a2[k].start()
        b2[k].start()
    o1.near()
    a2[0].near()
    b2[0].near()

    place = []
    at = 0
    for n, group in enumerate(GROUPS):
        size = 32 * len(group) + (64 if n == 2 else 0)
        place.append((at, size))
        at += size
    gid = [new_id() for _ in GROUPS]

    def rows_in(n):
        parts = [X[blk(*b)] for b in GROUPS[n]]
        if n == 2:
            parts += [XO[k] for k in range(4)]
        return jnp.concatenate(parts, axis=0)

    def up(n):
        lo, size = place[n]

        @pl.loop(0, 2 * FF // TILE)
        def _(t):
            cols = pl.ds(pl.multiple_of(t * TILE, TILE), TILE)
            acc = jnp.dot(rows_in(n), W[:, cols], preferred_element_type=F32)
            GU[lo:lo + size, cols] = acc
            GUs[lo:lo + size, cols] = acc.astype(BF16)

        v = pl.ds(lo, size)
        send(GUs.at[v], GUr.at[v], gid[n], sibling)

    def down(n):
        lo, size = place[n]
        take(GUr.at[pl.ds(lo, size)], gid[n], sibling)

        @pl.loop(0, size // 32)
        def _(t):
            r = pl.ds(pl.multiple_of(lo + t * 32, 32), 32)
            gate = GU[r, 0:FF] + GUr[r, 0:FF].astype(F32)
            upward = GU[r, FF:2 * FF] + GUr[r, FF:2 * FF].astype(F32)
            H[r, :] = (jax.nn.silu(gate) * upward).astype(BF16)

        @pl.loop(0, HALF // TILE)
        def _(t):
            cols = pl.ds(pl.multiple_of(t * TILE, TILE), TILE)
            acc = jnp.dot(H[lo:lo + size, :], Wd[:, cols], preferred_element_type=F32).astype(BF16)
            for i, b in enumerate(GROUPS[n]):
                Pb[blk(*b), :, cols] = acc[32 * i:32 * i + 32]
            if n == 2:
                base = 32 * len(GROUPS[n])
                for k in range(4):
                    PO[k, :, cols] = acc[base + 16 * k:base + 16 * k + 16]

    for copy in local[6:]:
        copy.wait()
    up(0)
    a1.far()
    a2[2].start()
    b1.far()
    b2[2].start()
    o1.far()
    XO[x] = jnp.concatenate([XOs[k] for k in range(4)], axis=0).astype(BF16)
    o2.start()
    for k in (1, -1):
        a2[k].near()
        b2[k].near()
    o2.near()
    a2[0].far()
    b2[0].far()
    up(1)
    a2[2].near()
    b2[2].near()
    down(0)
    for k in (1, -1):
        a2[k].far()
        b2[k].far()
    o2.far()
    a2[2].far()
    b2[2].far()
    up(2)
    down(1)
    down(2)

    def add_into(dst, srcs):
        n = dst.shape[-1]
        for j in range(n // 128):
            s = pl.ds(j * 128, 128)
            acc = dst[:, s].astype(F32)
            for src in srcs:
                acc = acc + src[:, s].astype(F32)
            dst[:, s] = acc.astype(dst.dtype)

    class Scatter:
        def __init__(self, axis, view, size, cut, dbuf, fbuf):
            self.view, self.size, self.cut = view, size, cut
            self.dev = {by: steps[axis](by) for by in (1, -1)}
            self.dp, self.dm, self.sp, self.sm = new_id(), new_id(), new_id(), new_id()
            self.d = (dbuf(0).at[:, pl.ds(0, cut)], dbuf(1).at[:, pl.ds(0, size - cut)])
            self.f = (fbuf(0), fbuf(1))

        def start(self):
            send(self.view(2, 0, self.cut), self.d[0], self.dp, self.dev[1])
            send(self.view(2, self.cut, self.size - self.cut), self.d[1], self.dm, self.dev[-1])

        def mid(self):
            take(self.d[0], self.dp, self.dev[1])
            add_into(self.view(1, 0, self.cut), [self.d[0]])
            send(self.view(1, 0, self.size), self.f[0], self.sp, self.dev[1])
            take(self.d[1], self.dm, self.dev[-1])
            add_into(self.view(-1, self.cut, self.size - self.cut), [self.d[1]])
            send(self.view(-1, 0, self.size), self.f[1], self.sm, self.dev[-1])

        def fin(self):
            take(self.f[0], self.sp, self.dev[1])
            take(self.f[1], self.sm, self.dev[-1])
            add_into(self.view(0, 0, self.size), self.f)

    ra1, rb1 = {}, {}
    for i, k in enumerate(order):
        ra1[k] = Scatter(
            "x", lambda r, lo, n, k=k: Pb.at[blk(r, k), :, pl.ds(lo, n)], FA, cut_a[k],
            lambda s, i=i: ad.at[i, s], lambda s, i=i: af.at[i, s],
        )
        rb1[k] = Scatter(
            "y", lambda r, lo, n, k=k: Pb.at[blk(k, r), :, pl.ds(FA + lo, n)], FB, cut_b[k],
            lambda s, i=i: bd.at[i, s], lambda s, i=i: bf.at[i, s],
        )
    ra2 = Scatter(
        "y", lambda r, lo, n: Pb.at[blk(0, r), :, pl.ds(lo, n)], FA, 640, lambda s: ad2.at[s], lambda s: af2.at[s]
    )
    rb2 = Scatter(
        "x", lambda r, lo, n: Pb.at[blk(r, 0), :, pl.ds(FA + lo, n)], FB, 896,
        lambda s: bd2.at[s], lambda s: bf2.at[s],
    )
    ro1 = Scatter(
        "x", lambda r, lo, n: PO.at[near(x, r), :, pl.ds(lo, n)], HALF, 1536, lambda s: od.at[s], lambda s: of.at[s]
    )
    ro2 = Scatter(
        "y", lambda r, lo, n: PS.at[near(y, r), :, pl.ds(lo, n)], HALF, 1536, lambda s: od2.at[s], lambda s: of2.at[s]
    )
    back = (2, 1, -1, 0)
    for k in back:
        ra1[k].start()
        rb1[k].start()
    ro1.start()
    for k in back:
        ra1[k].mid()
        rb1[k].mid()
    ro1.mid()
    ra1[2].fin()
    rb1[2].fin()
    ra2.start()
    rb2.start()
    for k in (1, -1):
        ra1[k].fin()
        rb1[k].fin()
    ra2.mid()
    rb2.mid()
    ro1.fin()
    own = PO[x].astype(F32)
    for k in range(4):
        PS[k] = own[4 * k:4 * k + 4]
    ro2.start()
    ra1[0].fin()
    rb1[0].fin()
    ro2.mid()
    ra2.fin()
    rb2.fin()
    ro2.fin()

    for n in range(4):
        at = lanes(n, 768)
        whole = Pb[here, :, at].astype(F32)
        for s in range(4):
            rzs[s, :, at] = whole[8 * s:8 * s + 8].astype(BF16)
    for s in range(4):
        rzos[s] = PS[y, s:s + 1, :]
    rid = [(new_id(), new_id()) for _ in range(3)]
    for k in (1, 3, 2):
        to = near(z, k)
        send(rzs.at[to], rzr.at[z], rid[k - 1][0], (c, chip(dz=k)))
        send(rzos.at[to], rzor.at[z], rid[k - 1][1], (c, chip(dz=k)))
    rzr[z] = rzs[z]
    rzor[z] = rzos[z]
    for k in (1, 3, 2):
        frm = near(z, -k)
        take(rzr.at[frm], rid[k - 1][0], (c, chip(dz=k)))
        take(rzor.at[frm], rid[k - 1][1], (c, chip(dz=k)))

    take0 = pick0[:, 0:48].astype(BF16)
    take1 = pick1[:, 0:48].astype(BF16)
    for n in range(4):
        at = lanes(n, 768)
        rows = jnp.concatenate(
            [rzr[e, :, at].astype(F32) for e in range(4)]
            + [rzor[e, :, at] for e in range(4)]
            + [jnp.zeros((12, 768), F32)],
            axis=0,
        ).astype(BF16)
        first = jnp.dot(take0, rows, preferred_element_type=F32)
        second = jnp.dot(take1, rows, preferred_element_type=F32)
        layer = (hb[:, at].astype(F32) + w0 * first + w1 * second).astype(out.dtype)
        layer = layer.astype(F32)
        for r in range(4):
            out[r, :, at] = layer[4 * r:4 * r + 4].astype(out.dtype)

    for copy in sent:
        copy.wait_send()


def shards(
    queries, cache_keys, cache_values, lengths, new_keys, new_values, residual, norm_gain,
    expert_ids, gate_logits, w_gate, w_up, w_down,
):
    hbm = pl.BlockSpec(memory_space=pl.ANY)
    vmem = pl.BlockSpec(memory_space=pltpu.VMEM)
    smem = pl.BlockSpec(memory_space=pltpu.SMEM)
    V = pltpu.VMEM
    rows = sum(32 * len(g) for g in GROUPS) + 64
    return pl.pallas_call(
        kernel,
        out_shape=jax.ShapeDtypeStruct((4, 4, HALF), BF16),
        in_specs=[smem, hbm, hbm, hbm, hbm, hbm, hbm, vmem, vmem, vmem, hbm, hbm, hbm],
        out_specs=vmem,
        scratch_shapes=[
            V((4, 4, HALF), BF16), V((4, 128, 512), BF16), V((4, 128, 512), BF16),
            V((4, 4, 512), BF16), V((4, 4, 512), BF16), V((4, 4, HALF), BF16),
            V((16, HALF), BF16), V((16, HALF), BF16), V((16, 128), F32), V((16, 128), F32),
            V((4, 8, HALF), BF16), V((4, 8, HALF), BF16), V((4, 1, HALF), F32), V((4, 1, HALF), F32),
            V((16, 32, HALF), BF16), V((4, 4, HALF), F32), V((4, 16, HALF), BF16),
            V((HALF, 2 * FF), BF16), V((FF, HALF), BF16),
            V((rows, 2 * FF), F32), V((rows, 2 * FF), BF16), V((rows, 2 * FF), BF16), V((rows, FF), BF16),
            V((16, 32, HALF), BF16), V((4, 16, HALF), BF16), V((4, 4, HALF), F32),
            V((4, 2, 32, 768), BF16), V((4, 2, 32, FA), BF16), V((2, 32, 768), BF16), V((2, 32, FA), BF16),
            V((4, 2, 32, 896), BF16), V((4, 2, 32, FB), BF16), V((2, 32, 896), BF16), V((2, 32, FB), BF16),
            V((2, 16, 1536), BF16), V((2, 16, HALF), BF16), V((2, 4, 1536), F32), V((2, 4, HALF), F32),
            V((4, 8, HALF), BF16), V((4, 8, HALF), BF16), V((4, 1, HALF), F32), V((4, 1, HALF), F32),
            pltpu.SemaphoreType.DMA((9,)), pltpu.SemaphoreType.DMA((NSEM,)), pltpu.SemaphoreType.DMA((NSEM,)),
        ],
        compiler_params=pltpu.CompilerParams(collective_id=0, has_side_effects=True),
        name="layer",
    )(
        lengths, queries, cache_keys, cache_values, new_keys, new_values, residual,
        norm_gain.reshape(48, 128), expert_ids, gate_logits, w_gate, w_up, w_down,
    )


def solution(mesh):
    return jax.shard_map(
        shards,
        mesh=mesh,
        in_specs=(
            P("dev", None, None),
            P("dev", None, None),
            P("dev", None, None),
            P("dev"),
            P("dev", None, None),
            P("dev", None, None),
            P("dev", None, None),
            P(),
            P("dev", None),
            P("dev", None),
            P(None, "dev"),
            P(None, "dev"),
            P("dev", None),
        ),
        out_specs=P("dev", None, "sec"),
        check_vma=False,
    )
```

time: 404 us -> 85 us (0.21)
  waiting for transfers between devices: 312 us -> 0 us
  Pallas kernels: 0 us -> 79.4 us
  starting transfers between devices: 37.8 us -> 0 us
  local copies, waits for them, and re-layouts: 19.7 us -> 4.27 us
  between operations: 13.5 us -> 0.01 us
  other arithmetic: 12.6 us -> 0 us
  matrix products: 4.7 us -> 0 us
    all_to_all x1 -> x0, waiting for transfers between devices: 165 us -> none  [shards(): lax.all_to_all(partials, 'dev', split_axis=0, concat_axis=0, tiled=True)]
    all_gather x1 -> x0, waiting for transfers between devices: 144 us -> none  [shards(): lax.all_gather(moved_rows, 'dev', axis=1, tiled=True)]
    pallas_call x0 -> x1, Pallas kernels: none -> 79.4 us  [shards(): pl.pallas_call(kernel, out_shape=jax.ShapeDtypeStruct((4, 4, HALF), BF16)...]
    ppermute x3 -> x0, starting transfers between devices: 28.6 us -> none  [from_behind(): return lax.ppermute(x, axis, pairs)]
    reshape x11 -> x0, local copies, waits for them, and re-layouts: 14.1 us -> none  [the longest x1 10.2 us: shards(): partials = partials.reshape(devices, CAP, width)]
    all_to_all x1 -> x0, starting transfers between devices: 9.15 us -> none  [shards(): lax.all_to_all(partials, 'dev', split_axis=0, concat_axis=0, tiled=True)]
    reduce_sum x4 -> x0, other arithmetic: 7.93 us -> none  [the longest x1 6.85 us: shards(): jnp.sum(returned.reshape(EXP, group, CAP, width).astype(jnp.float32), axi...]
  transfers between devices with their start and end apart: 5 -> 0, of which waited for: 4 -> 0; matrix products, arithmetic and copies ran while one was open for 0% -> 0% of each run, Pallas kernels for 0% -> 0%
where the time goes in v1:
time: 85 us; the launch traced here: 83.6 us
  Pallas kernels  79.4 us (93%)
  local copies, waits for them, and re-layouts  4.27 us (5%)
    pallas_call x1, Pallas kernels, shards(): pl.pallas_call(kernel, out_shape=jax.ShapeDtypeStruct((4, 4, HALF), BF16)...  79.4 us
    unnamed x3, local copies, waits for them, and re-layouts  4.27 us

profile of v1, /device:TPU:32, one launch (start us, length us, event | category | flops | bytes accessed | tf_op | source)
XLA Modules:
  0.0 83.6 jit_solution(7177983246589444619)
XLA Ops:
  0.0 1.4 %copy.14.ids = s32[16,2]{1,0:T(8,128)} copy(s32[16,2]{0,1:T(2,128)} %param.21) | data formatting | bytes 256 | tf_op args[8]
  1.4 1.3 %copy.15.logits = f32[16,2]{1,0:T(8,128)} copy(f32[16,2]{0,1:T(2,128)} %param.22) | data formatting | bytes 256 | tf_op args[9]
  2.7 79.4 %layer.1 = bf16[4,4,3072]{2,1,0:T(4,128)(2,1)} custom-call(s32[4]{0:T(128)} %lens.1, bf16[4,4,6144]{2,1,0:T(4,128)(2,1)} %q_hbm.1, bf16[4,128,1024]{2,1,0:T(8,128)(2,1)} %k_hbm.1, bf16[4,128,1024]{2,1,0:T(8,128)(2,1)} %v_hbm.1, bf16[4,4,1024]{2,1,0:T(4,128)(2,1)} %nk_hbm.1, bf16[4,4,1024]{2,1,0:T(4,128)(2,1)} %nv_hbm.1, bf16[4,4,6144]{2,1,0:T(4,128)(2,1)} %res_hbm.1, ...), custom_call_target="tpu_custom_call" | custom-call | tf_op jit(solution)/shard_map/layer/pallas_call | solution.py:480
  82.1 1.6 %copy.17 = bf16[4,4,3072]{2,1,0:T(4,128)(2,1)} copy(bf16[4,4,3072]{2,1,0:T(4,128)(2,1)} %layer.1) | data formatting | bytes 196608

commit v2 on v1

v2 whole, which is shorter than its diff:
```python
import jax
import jax.numpy as jnp
from jax import lax
from jax.experimental import pallas as pl
from jax.experimental.pallas import tpu as pltpu
from jax.sharding import PartitionSpec as P

HD = 128
EPS = 1e-05

F32 = jnp.float32
BF16 = jnp.bfloat16
HALF = 3072
FF = 512
NSEM = 288
TILE = 256
WAVES = 2
FA = (1536, 1280)
CUT_A = (768, 640)
CUT_B = (768, 896)
ORDER = (0, 1, -1, 2)
BLOCKS = tuple((i, j) for i in range(4) for j in range(4))


def lanes(j, n=128):
    return slice(j * n, (j + 1) * n)


def kernel(
    lens, q_hbm, k_hbm, v_hbm, nk_hbm, nv_hbm, res_hbm, gain, ids, logits, wg_hbm, wu_hbm, wd_hbm,
    out,
    qb, kb, vb, nkb, nvb, resb, hb, xn, ssb, ssr,
    zs, zr, zos, zor, X, XOs, XO, W, Wd, GU, GUs, GUr, H, Pb, PO, PS,
    ad, af, ad2, af2, bd, bf, bd2, bf2, od, of, od2, of2, rzs, rzr, rzos, rzor,
    lsem, ssem, rsem,
):
    c = lax.axis_index("sec")
    d = lax.axis_index("dev")
    z = d // 16
    x = (d // 4) % 4
    y = d % 4
    here = x * 4 + y

    def near(v, by):
        return lax.rem(v + (by % 4), 4)

    def chip(dz=0, dx=0, dy=0):
        return near(z, dz) * 16 + near(x, dx) * 4 + near(y, dy)

    steps = {"x": lambda by: (c, chip(dx=by)), "y": lambda by: (c, chip(dy=by))}
    zpeers = [(c, chip(dz=k)) for k in (1, 2, 3)]
    sibling = (1 - c, d)
    partners = zpeers + [sibling] + [steps[a](by) for a in ("x", "y") for by in (1, -1)]

    barrier = pltpu.get_barrier_semaphore()
    for p in partners:
        pl.semaphore_signal(barrier, inc=1, device_id=p, device_id_type=pl.DeviceIdType.MESH)

    feats = pl.ds(pl.multiple_of(c * HALF, HALF), HALF)
    kvs = pl.ds(pl.multiple_of(c * 512, 512), 512)
    local = []
    for i, (src, dst) in enumerate((
        (q_hbm.at[:, :, feats], qb),
        (k_hbm.at[:, :, kvs], kb),
        (nk_hbm.at[:, :, kvs], nkb),
        (v_hbm.at[:, :, kvs], vb),
        (nv_hbm.at[:, :, kvs], nvb),
        (res_hbm.at[:, :, feats], resb),
        (wg_hbm.at[feats, :], W.at[:, pl.ds(0, FF)]),
        (wu_hbm.at[feats, :], W.at[:, pl.ds(FF, FF)]),
        (wd_hbm.at[:, feats], Wd),
    )):
        copy = pltpu.make_async_copy(src, dst, lsem.at[i])
        copy.start()
        local.append(copy)

    counter = [0]
    sent = []

    def new_id():
        counter[0] += 1
        return counter[0] - 1

    def send(src, dst, sem, dev):
        copy = pltpu.make_async_remote_copy(
            src_ref=src, dst_ref=dst, send_sem=ssem.at[sem], recv_sem=rsem.at[sem],
            device_id=dev, device_id_type=pl.DeviceIdType.MESH,
        )
        copy.start()
        sent.append(copy)

    def take(dst, sem, dev):
        pltpu.make_async_remote_copy(
            src_ref=dst, dst_ref=dst, send_sem=ssem.at[sem], recv_sem=rsem.at[sem],
            device_id=dev, device_id_type=pl.DeviceIdType.MESH,
        ).wait_recv()

    square = (16, 16)
    down_row = lax.broadcasted_iota(jnp.int32, square, 0)
    across = lax.broadcasted_iota(jnp.int32, square, 1)

    def column(ref, k):
        rows = jnp.broadcast_to(ref[k:k + 1, :], square)
        return jnp.sum(jnp.where(down_row == across, rows, jnp.zeros_like(rows)), axis=1, keepdims=True)

    id0, id1 = column(ids, 0), column(ids, 1)
    slot = lax.broadcasted_iota(jnp.int32, (16, 128), 1)
    who = jnp.where(slot < 32, slot // 8, slot - 32)
    rank = jnp.where(slot < 32, slot % 8, 8)
    hit0 = id0 == who
    hit1 = id1 == who
    hit = jnp.where(hit0 | hit1, 1.0, 0.0)
    before = jnp.where(across < down_row, 1.0, 0.0)
    ahead = jnp.dot(before.astype(BF16), hit.astype(BF16), preferred_element_type=F32)
    chosen = ahead == rank.astype(F32)
    pick0 = jnp.where(hit0 & chosen, 1.0, 0.0)
    pick1 = jnp.where(hit1 & chosen, 1.0, 0.0)
    packing = jnp.transpose(pick0 + pick1)[0:48].astype(BF16)
    l0, l1 = column(logits, 0), column(logits, 1)
    top = jnp.maximum(l0, l1)
    e0, e1 = jnp.exp(l0 - top), jnp.exp(l1 - top)
    w0 = e0 / (e0 + e1)
    w1 = e1 / (e0 + e1)

    for copy in local[:6]:
        copy.wait()
    row = lax.broadcasted_iota(jnp.int32, (96, 128), 0)
    col = lax.broadcasted_iota(jnp.int32, (96, 128), 1)
    lenv = jnp.concatenate([jnp.full((24, 128), lens[r], jnp.int32) for r in range(4)], axis=0)
    in_cache = col < lenv
    row16 = lax.broadcasted_iota(jnp.int32, (96, 16), 0)
    col16 = lax.broadcasted_iota(jnp.int32, (96, 16), 1)
    in_window = (row16 // 24 == col16 // 4) & (col16 % 4 <= row16 % 4)
    scale = HD ** (-0.5)
    ss = jnp.zeros((16, 128), F32)
    contract = (((1,), (1,)), ((), ()))
    for g in range(4):
        qs = [
            jnp.concatenate([qb[r, :, lanes(g * 6 + h)].astype(F32) for h in range(6)], axis=0)
            for r in range(4)
        ]
        sc = jnp.concatenate([
            lax.dot_general(qs[r].astype(BF16), kb[r, :, lanes(g)], contract, preferred_element_type=F32)
            for r in range(4)
        ], axis=0) * scale
        nk = jnp.concatenate([nkb[r, :, lanes(g)].astype(F32) for r in range(4)], axis=0).astype(BF16)
        nv = jnp.concatenate([nvb[r, :, lanes(g)].astype(F32) for r in range(4)], axis=0).astype(BF16)
        qa = jnp.concatenate(qs, axis=0).astype(BF16)
        sn = lax.dot_general(qa, nk, contract, preferred_element_type=F32) * scale
        sc = jnp.where(in_cache, sc, -1e30)
        sn = jnp.where(in_window, sn, -1e30)
        peak = jnp.maximum(jnp.max(sc, axis=1, keepdims=True), jnp.max(sn, axis=1, keepdims=True))
        ec = jnp.exp(sc - peak)
        en = jnp.exp(sn - peak)
        total = jnp.sum(ec, axis=1, keepdims=True) + jnp.sum(en, axis=1, keepdims=True)
        inv = 1.0 / total
        pc = ec * inv
        pn = (en * inv).astype(BF16)
        att = jnp.concatenate([
            jnp.dot(pc[24 * r:24 * r + 24].astype(BF16), vb[r, :, lanes(g)], preferred_element_type=F32)
            for r in range(4)
        ], axis=0) + jnp.dot(pn, nv, preferred_element_type=F32)
        for h in range(6):
            j = g * 6 + h
            part = jnp.concatenate([att[r * 24 + h * 4:r * 24 + h * 4 + 4] for r in range(4)], axis=0)
            res = jnp.concatenate([resb[r, :, lanes(j)].astype(F32) for r in range(4)], axis=0)
            hst = (res + part).astype(BF16)
            hb[:, lanes(j)] = hst
            hf = hst.astype(F32)
            ss = ss + hf * hf
    ssb[...] = jnp.broadcast_to(jnp.sum(ss, axis=1, keepdims=True), (16, 128))
    pl.semaphore_wait(barrier, len(partners))
    sid = new_id()
    send(ssb, ssr, sid, sibling)

    take(ssr, sid, sibling)
    inv = lax.rsqrt((ssb[...] + ssr[...]) / (2 * HALF) + EPS)
    gains = gain[pl.ds(pl.multiple_of(c * 24, 8), 24), :]
    for j in range(24):
        xn[:, lanes(j)] = (hb[:, lanes(j)].astype(F32) * inv * gains[j:j + 1]).astype(BF16)
    for n in range(4):
        at = lanes(n, 768)
        packed = jnp.dot(packing, xn[:, at], preferred_element_type=F32)
        for e in range(4):
            zs[e, :, at] = packed[8 * e:8 * e + 8].astype(BF16)
            zos[e, :, at] = packed[32 + e:33 + e]

    zid = {k: (new_id(), new_id()) for k in (1, 3, 2)}
    for k in (1, 3, 2):
        send(zs.at[near(z, k)], zr.at[k], zid[k][0], (c, chip(dz=k)))
    for k in (1, 3, 2):
        send(zos.at[near(z, k)], zor.at[k], zid[k][1], (c, chip(dz=k)))

    def form(w, first, second):
        for n in range(4):
            at = lanes(n, 768)
            X[w, here, :, at] = jnp.concatenate([first(at).astype(F32), second(at).astype(F32)], axis=0).astype(BF16)

    take(zr.at[1], zid[1][0], (c, chip(dz=1)))
    form(0, lambda at: zs[z, :, at], lambda at: zr[1, :, at])

    def second_wave():
        for k in (3, 2):
            take(zr.at[k], zid[k][0], (c, chip(dz=k)))
        form(1, lambda at: zr[3, :, at], lambda at: zr[2, :, at])
        for k in (1, 3, 2):
            take(zor.at[k], zid[k][1], (c, chip(dz=k)))
        XOs[y, 0:1, :] = zos[z]
        for k in (1, 2, 3):
            XOs[y, k:k + 1, :] = zor[k]

    def blk(dx, dy):
        return near(x, dx) * 4 + near(y, dy)

    class Gather:
        def __init__(self, axis, view, size, cut):
            self.one = lambda r: view(r, 0, cut)
            self.two = lambda r: view(r, cut, size - cut)
            self.dev = {by: steps[axis](by) for by in (1, -1)}
            self.id = [new_id() for _ in range(6)]

        def start(self):
            one, two = self.one(0), self.two(0)
            send(one, one, self.id[0], self.dev[1])
            send(two, two, self.id[1], self.dev[-1])
            send(two, two, self.id[2], self.dev[1])
            send(one, one, self.id[3], self.dev[-1])

        def pass_on(self):
            v = self.one(-1)
            take(v, self.id[0], self.dev[1])
            send(v, v, self.id[4], self.dev[1])
            v = self.two(1)
            take(v, self.id[1], self.dev[-1])
            send(v, v, self.id[5], self.dev[-1])

        def rest(self):
            take(self.two(-1), self.id[2], self.dev[1])
            take(self.one(1), self.id[3], self.dev[-1])

        def far(self):
            take(self.one(2), self.id[4], self.dev[1])
            take(self.two(2), self.id[5], self.dev[-1])

    def gathers(w):
        fa, ca, cb = FA[w], CUT_A[w], CUT_B[w]
        fb = HALF - fa
        Xw = X.at[w]
        a1 = Gather("y", lambda r, lo, n: Xw.at[blk(0, r), :, pl.ds(lo, n)], fa, ca)
        b1 = Gather("x", lambda r, lo, n: Xw.at[blk(r, 0), :, pl.ds(fa + lo, n)], fb, cb)
        a2 = {
            k: Gather("x", lambda r, lo, n, k=k: Xw.at[blk(r, k), :, pl.ds(lo, n)], fa, ca) for k in ORDER
        }
        b2 = {
            k: Gather("y", lambda r, lo, n, k=k: Xw.at[blk(k, r), :, pl.ds(fa + lo, n)], fb, cb) for k in ORDER
        }
        if w == 1:
            o1 = Gather("y", lambda r, lo, n: XOs.at[near(y, r), :, pl.ds(lo, n)], HALF, HALF // 2)
            o2 = Gather("x", lambda r, lo, n: XO.at[near(x, r), :, pl.ds(lo, n)], HALF, HALF // 2)

        def start():
            a1.start()
            b1.start()
            if w == 1:
                o1.start()
            a2[0].start()
            b2[0].start()

        def line():
            a1.pass_on()
            b1.pass_on()
            a1.rest()
            a2[1].start()
            b1.rest()
            b2[1].start()
            a2[-1].start()
            b2[-1].start()

        def line_over():
            o1.pass_on()
            o1.rest()

        def own():
            a2[0].pass_on()
            b2[0].pass_on()

        def far_line():
            a1.far()
            a2[2].start()
            b1.far()
            b2[2].start()

        def over():
            o1.far()
            XO[x] = jnp.concatenate([XOs[k] for k in range(4)], axis=0).astype(BF16)
            o2.start()

        def sides(k):
            a2[k].pass_on()
            b2[k].pass_on()

        def over_pass():
            o2.pass_on()

        def finish():
            for k in ORDER:
                a2[k].rest()
                b2[k].rest()
                a2[k].far()
                b2[k].far()
            if w == 1:
                o2.rest()
                o2.far()

        steps_of = [start, line, own, far_line, lambda: sides(1), lambda: sides(-1), lambda: sides(2), finish]
        if w == 1:
            steps_of = [
                start, line, line_over, own, far_line, over, lambda: sides(1), lambda: sides(-1), lambda: sides(2),
                over_pass, finish,
            ]
        return steps_of

    place = ((0, 256), (256, 320))
    gid = [[[new_id(), new_id()] for _ in range(2)] for _ in range(WAVES)]

    def experts(w):
        lo, size = place[w]
        v = pl.ds(lo, size)

        def rows():
            parts = [X[w, k] for k in range(16)]
            if w == 1:
                parts += [XO[k] for k in range(4)]
            return jnp.concatenate(parts, axis=0)

        def up(t):
            cols = pl.ds(t * TILE, TILE)
            acc = jnp.dot(rows(), W[:, cols], preferred_element_type=F32)
            GU[v, cols] = acc
            GUs[v, cols] = acc.astype(BF16)

        def up_half(h):
            up(h)
            up(h + 2)
            for i, t in enumerate((h, h + 2)):
                cols = pl.ds(t * TILE, TILE)
                send(GUs.at[v, cols], GUr.at[v, cols], gid[w][h][i], sibling)

        def hidden(h):
            for i, t in enumerate((h, h + 2)):
                take(GUr.at[v, pl.ds(t * TILE, TILE)], gid[w][h][i], sibling)
            one = pl.ds(h * TILE, TILE)
            two = pl.ds(FF + h * TILE, TILE)

            @pl.loop(0, size // 32)
            def _(i):
                r = pl.ds(pl.multiple_of(lo + i * 32, 32), 32)
                gate = GU[r, one] + GUr[r, one].astype(F32)
                upward = GU[r, two] + GUr[r, two].astype(F32)
                H[r, one] = (jax.nn.silu(gate) * upward).astype(BF16)

        def down(t):
            cols = pl.ds(t * TILE, TILE)
            acc = jnp.dot(H[v, :], Wd[:, cols], preferred_element_type=F32).astype(BF16)
            for k in range(16):
                Pb[w, k, :, cols] = acc[16 * k:16 * k + 16]
            if w == 1:
                for k in range(4):
                    PO[k, :, cols] = acc[256 + 16 * k:272 + 16 * k]

        return (
            [lambda: up_half(0), lambda: up_half(1), lambda: hidden(0), lambda: hidden(1)]
            + [lambda t=t: (down(2 * t), down(2 * t + 1)) for t in range(6)]
        )

    def add_into(dst, srcs):
        n = dst.shape[-1]
        for j in range(n // 128):
            s = pl.ds(j * 128, 128)
            acc = dst[:, s].astype(F32)
            for src in srcs:
                acc = acc + src[:, s].astype(F32)
            dst[:, s] = acc.astype(dst.dtype)

    class Scatter:
        def __init__(self, axis, view, size, cut, dbuf, fbuf):
            self.one = lambda r: view(r, 0, cut)
            self.two = lambda r: view(r, cut, size - cut)
            self.whole = lambda r: view(r, 0, size)
            self.dev = {by: steps[axis](by) for by in (1, -1)}
            self.id = [new_id() for _ in range(6)]
            self.d = (dbuf(0).at[:, pl.ds(0, cut)], dbuf(1).at[:, pl.ds(0, size - cut)])
            self.f = (fbuf(0), fbuf(1))
            self.f1 = [f.at[:, pl.ds(0, cut)] for f in self.f]
            self.f2 = [f.at[:, pl.ds(cut, size - cut)] for f in self.f]

        def start(self):
            send(self.one(2), self.d[0], self.id[0], self.dev[1])
            send(self.two(2), self.d[1], self.id[1], self.dev[-1])

        def plain(self):
            send(self.two(1), self.f2[0], self.id[2], self.dev[1])
            send(self.one(-1), self.f1[1], self.id[3], self.dev[-1])

        def mid(self):
            take(self.d[0], self.id[0], self.dev[1])
            add_into(self.one(1), [self.d[0]])
            send(self.one(1), self.f1[0], self.id[4], self.dev[1])
            take(self.d[1], self.id[1], self.dev[-1])
            add_into(self.two(-1), [self.d[1]])
            send(self.two(-1), self.f2[1], self.id[5], self.dev[-1])

        def fin(self):
            take(self.f2[0], self.id[2], self.dev[1])
            take(self.f1[1], self.id[3], self.dev[-1])
            take(self.f1[0], self.id[4], self.dev[1])
            take(self.f2[1], self.id[5], self.dev[-1])
            add_into(self.whole(0), self.f)

    rid = {k: (new_id(), new_id()) for k in (1, 2, 3)}

    def scatters(w):
        fa, ca, cb = FA[w], CUT_A[w], CUT_B[w]
        fb = HALF - fa
        Pw = Pb.at[w]
        wa, wb = pl.ds(0, fa), pl.ds(0, fb)
        a1, b1 = {}, {}
        for i, k in enumerate(ORDER):
            a1[k] = Scatter(
                "x", lambda r, lo, n, k=k: Pw.at[blk(r, k), :, pl.ds(lo, n)], fa, ca,
                lambda s, i=i: ad.at[w, i, s], lambda s, i=i: af.at[w, i, s, :, wa],
            )
            b1[k] = Scatter(
                "y", lambda r, lo, n, k=k: Pw.at[blk(k, r), :, pl.ds(fa + lo, n)], fb, cb,
                lambda s, i=i: bd.at[w, i, s], lambda s, i=i: bf.at[w, i, s, :, wb],
            )
        a2 = Scatter(
            "y", lambda r, lo, n: Pw.at[blk(0, r), :, pl.ds(lo, n)], fa, ca,
            lambda s: ad2.at[w, s], lambda s: af2.at[w, s, :, wa],
        )
        b2 = Scatter(
            "x", lambda r, lo, n: Pw.at[blk(r, 0), :, pl.ds(fa + lo, n)], fb, cb,
            lambda s: bd2.at[w, s], lambda s: bf2.at[w, s, :, wb],
        )
        if w == 1:
            o1 = Scatter(
                "x", lambda r, lo, n: PO.at[near(x, r), :, pl.ds(lo, n)], HALF, HALF // 2,
                lambda s: od.at[s], lambda s: of.at[s],
            )
            o2 = Scatter(
                "y", lambda r, lo, n: PS.at[near(y, r), :, pl.ds(lo, n)], HALF, HALF // 2,
                lambda s: od2.at[s], lambda s: of2.at[s],
            )
        back = (2, 1, -1, 0)

        def start():
            if w == 1:
                o1.start()
            for k in back:
                a1[k].start()
                b1[k].start()
            if w == 1:
                o1.plain()
            for k in back:
                a1[k].plain()
                b1[k].plain()

        def over_mid():
            o1.mid()

        def mid(k):
            a1[k].mid()
            b1[k].mid()

        def far():
            a1[2].fin()
            a2.start()
            b1[2].fin()
            b2.start()

        def over():
            o1.fin()
            own = PO[x].astype(F32)
            for k in range(4):
                PS[k] = own[4 * k:4 * k + 4]
            o2.start()
            o2.plain()

        def sides():
            for k in (1, -1):
                a1[k].fin()
                b1[k].fin()
            a2.plain()
            b2.plain()

        def cross():
            a2.mid()
            b2.mid()

        def over_cross():
            o2.mid()

        def finish():
            a1[0].fin()
            b1[0].fin()
            a2.fin()
            b2.fin()
            if w == 1:
                o2.fin()

        def home():
            for n in range(4):
                at = lanes(n, 768)
                whole = Pw[here, :, at].astype(F32)
                rzs[w, 0, :, at] = whole[0:8].astype(BF16)
                rzs[w, 1, :, at] = whole[8:16].astype(BF16)
            if w == 0:
                send(rzs.at[0, 1], rzr.at[3], rid[3][0], (c, chip(dz=-1)))
            else:
                send(rzs.at[1, 1], rzr.at[2], rid[2][0], (c, chip(dz=2)))
                send(rzs.at[1, 0], rzr.at[1], rid[1][0], (c, chip(dz=1)))
                for s in range(4):
                    rzos[s] = PS[y, s:s + 1, :]
                for s, k in ((2, 2), (1, 3), (3, 1)):
                    send(rzos.at[s], rzor.at[k], rid[k][1], (c, chip(dz=k)))

        if w == 0:
            return [start] + [lambda k=k: mid(k) for k in back] + [far, sides, cross, finish, home]
        return (
            [start, over_mid] + [lambda k=k: mid(k) for k in back]
            + [over, far, sides, over_cross, cross, finish, home]
        )

    g0, g1 = gathers(0), gathers(1)
    x0, x1 = experts(0), experts(1)
    s0, s1 = scatters(0), scatters(1)

    def run(*todo):
        for f in todo:
            f()

    run(*g0[:4])
    second_wave()
    run(*g0[4:6])
    run(g1[0])
    run(*g0[6:])
    for copy in local[6:]:
        copy.wait()
    run(g1[1], x0[0], g1[2], g1[3], x0[1], g1[4], g1[5], x0[2], x0[3], g1[6])
    run(x0[4], x0[5], g1[7], x0[6], x0[7], g1[8], x0[8], x0[9])
    run(g1[9], s0[0], g1[10])
    run(x1[0], s0[1], s0[2], x1[1], s0[3], s0[4], x1[2], x1[3], s0[5], s0[6])
    run(x1[4], x1[5], s0[7], x1[6], x1[7], x1[8], x1[9])
    run(s1[0], s0[8], s0[9])
    run(*s1[1:])

    rzr[0] = rzs[0, 0]
    rzor[0] = rzos[0]
    for k in (3, 1, 2):
        take(rzr.at[k], rid[k][0], (c, chip(dz=k)))
        take(rzor.at[k], rid[k][1], (c, chip(dz=k)))
    take0 = pick0[:, 0:48].astype(BF16)
    take1 = pick1[:, 0:48].astype(BF16)
    behind = [lax.rem(z - e + 4, 4) for e in range(4)]
    for n in range(4):
        at = lanes(n, 768)
        rows = jnp.concatenate(
            [rzr[behind[e], :, at].astype(F32) for e in range(4)]
            + [rzor[behind[e], :, at] for e in range(4)]
            + [jnp.zeros((12, 768), F32)],
            axis=0,
        ).astype(BF16)
        first = jnp.dot(take0, rows, preferred_element_type=F32)
        second = jnp.dot(take1, rows, preferred_element_type=F32)
        layer = hb[:, at].astype(F32) + w0 * first + w1 * second
        for r in range(4):
            out[r, :, at] = layer[4 * r:4 * r + 4].astype(out.dtype)

    assert counter[0] <= NSEM
    for copy in sent:
        copy.wait_send()


def shards(
    queries, cache_keys, cache_values, lengths, new_keys, new_values, residual, norm_gain,
    expert_ids, gate_logits, w_gate, w_up, w_down,
):
    hbm = pl.BlockSpec(memory_space=pl.ANY)
    vmem = pl.BlockSpec(memory_space=pltpu.VMEM)
    smem = pl.BlockSpec(memory_space=pltpu.SMEM)
    V = pltpu.VMEM
    rows = 576
    return pl.pallas_call(
        kernel,
        out_shape=jax.ShapeDtypeStruct((4, 4, HALF), BF16),
        in_specs=[smem, hbm, hbm, hbm, hbm, hbm, hbm, vmem, vmem, vmem, hbm, hbm, hbm],
        out_specs=vmem,
        scratch_shapes=[
            V((4, 4, HALF), BF16), V((4, 128, 512), BF16), V((4, 128, 512), BF16),
            V((4, 4, 512), BF16), V((4, 4, 512), BF16), V((4, 4, HALF), BF16),
            V((16, HALF), BF16), V((16, HALF), BF16), V((16, 128), F32), V((16, 128), F32),
            V((4, 8, HALF), BF16), V((4, 8, HALF), BF16), V((4, 1, HALF), F32), V((4, 1, HALF), F32),
            V((WAVES, 16, 16, HALF), BF16), V((4, 4, HALF), F32), V((4, 16, HALF), BF16),
            V((HALF, 2 * FF), BF16), V((FF, HALF), BF16),
            V((rows, 2 * FF), F32), V((rows, 2 * FF), BF16), V((rows, 2 * FF), BF16), V((rows, FF), BF16),
            V((WAVES, 16, 16, HALF), BF16), V((4, 16, HALF), BF16), V((4, 4, HALF), F32),
            V((WAVES, 4, 2, 16, 768), BF16), V((WAVES, 4, 2, 16, 1536), BF16),
            V((WAVES, 2, 16, 768), BF16), V((WAVES, 2, 16, 1536), BF16),
            V((WAVES, 4, 2, 16, 896), BF16), V((WAVES, 4, 2, 16, 1792), BF16),
            V((WAVES, 2, 16, 896), BF16), V((WAVES, 2, 16, 1792), BF16),
            V((2, 16, 1536), BF16), V((2, 16, HALF), BF16), V((2, 4, 1536), F32), V((2, 4, HALF), F32),
            V((WAVES, 2, 8, HALF), BF16), V((4, 8, HALF), BF16), V((4, 1, HALF), F32), V((4, 1, HALF), F32),
            pltpu.SemaphoreType.DMA((9,)), pltpu.SemaphoreType.DMA((NSEM,)), pltpu.SemaphoreType.DMA((NSEM,)),
        ],
        compiler_params=pltpu.CompilerParams(collective_id=0, has_side_effects=True),
        name="layer",
    )(
        lengths, queries, cache_keys, cache_values, new_keys, new_values, residual,
        norm_gain.reshape(48, 128), expert_ids.T, gate_logits.T, w_gate, w_up, w_down,
    )


def solution(mesh):
    return jax.shard_map(
        shards,
        mesh=mesh,
        in_specs=(
            P("dev", None, None),
            P("dev", None, None),
            P("dev", None, None),
            P("dev"),
            P("dev", None, None),
            P("dev", None, None),
            P("dev", None, None),
            P(),
            P("dev", None),
            P("dev", None),
            P(None, "dev"),
            P(None, "dev"),
            P("dev", None),
        ),
        out_specs=P("dev", None, "sec"),
        check_vma=False,
    )
```

time: 85 us -> 80 us (0.941); the launches traced: 83.6 us -> 79.8 us
  local copies, waits for them, and re-layouts: 4.27 us -> 1.57 us
  Pallas kernels: 79.4 us -> 78.2 us
    unnamed x3 -> x1, local copies, waits for them, and re-layouts: 4.27 us -> 1.57 us
    pallas_call x1, Pallas kernels: 79.4 us -> 78.2 us  [shards(): pl.pallas_call(kernel, out_shape=jax.ShapeDtypeStruct((4, 4, HALF), BF16)...]
where the time goes in v2:
time: 80 us; the launch traced here: 79.8 us
  Pallas kernels  78.2 us (98%)
  local copies, waits for them, and re-layouts  1.57 us (2%)
    pallas_call x1, Pallas kernels, shards(): pl.pallas_call(kernel, out_shape=jax.ShapeDtypeStruct((4, 4, HALF), BF16)...  78.2 us

profile of v2, /device:TPU:32, one launch (start us, length us, event | category | flops | bytes accessed | tf_op | source)
XLA Modules:
  0.0 79.8 jit_solution(5647244956566280969)
XLA Ops:
  0.0 78.2 %layer.1 = bf16[4,4,3072]{2,1,0:T(4,128)(2,1)} custom-call(s32[4]{0:T(128)} %lens.1, bf16[4,4,6144]{2,1,0:T(4,128)(2,1)} %q_hbm.1, bf16[4,128,1024]{2,1,0:T(8,128)(2,1)} %k_hbm.1, bf16[4,128,1024]{2,1,0:T(8,128)(2,1)} %v_hbm.1, bf16[4,4,1024]{2,1,0:T(4,128)(2,1)} %nk_hbm.1, bf16[4,4,1024]{2,1,0:T(4,128)(2,1)} %nv_hbm.1, bf16[4,4,6144]{2,1,0:T(4,128)(2,1)} %res_hbm.1, ...), custom_call_target="tpu_custom_call" | custom-call | tf_op jit(solution)/shard_map/layer/pallas_call | solution.py:593
  78.2 1.6 %copy.15 = bf16[4,4,3072]{2,1,0:T(4,128)(2,1)} copy(bf16[4,4,3072]{2,1,0:T(4,128)(2,1)} %layer.1) | data formatting | bytes 196608

commit v3 on v2

--- a/solution.py
+++ b/solution.py
@@ -29,7 +29,7 @@
 def kernel(
     lens, q_hbm, k_hbm, v_hbm, nk_hbm, nv_hbm, res_hbm, gain, ids, logits, wg_hbm, wu_hbm, wd_hbm,
     out,
-    qb, kb, vb, nkb, nvb, resb, hb, xn, ssb, ssr,
+    ob, qb, kb, vb, nkb, nvb, resb, hb, xn, ssb, ssr,
     zs, zr, zos, zor, X, XOs, XO, W, Wd, GU, GUs, GUr, H, Pb, PO, PS,
     ad, af, ad2, af2, bd, bf, bd2, bf2, od, of, od2, of2, rzs, rzr, rzos, rzor,
     lsem, ssem, rsem,
@@ -71,11 +71,13 @@
         (wd_hbm.at[:, feats], Wd),
     )):
         copy = pltpu.make_async_copy(src, dst, lsem.at[i])
-        copy.start()
+        if i < 6:
+            copy.start()
         local.append(copy)
 
     counter = [0]
     sent = []
+    flushed = [0]
 
     def new_id():
         counter[0] += 1
@@ -88,6 +90,11 @@
         )
         copy.start()
         sent.append(copy)
+
+    def flush(upto):
+        for copy in sent[flushed[0]:upto]:
+            copy.wait_send()
+        flushed[0] = max(flushed[0], upto)
 
     def take(dst, sem, dev):
         pltpu.make_async_remote_copy(
@@ -124,6 +131,8 @@
 
     for copy in local[:6]:
         copy.wait()
+    for copy in local[6:]:
+        copy.start()
     row = lax.broadcasted_iota(jnp.int32, (96, 128), 0)
     col = lax.broadcasted_iota(jnp.int32, (96, 128), 1)
     lenv = jnp.concatenate([jnp.full((24, 128), lens[r], jnp.int32) for r in range(4)], axis=0)
@@ -548,11 +557,21 @@
         copy.wait()
     run(g1[1], x0[0], g1[2], g1[3], x0[1], g1[4], g1[5], x0[2], x0[3], g1[6])
     run(x0[4], x0[5], g1[7], x0[6], x0[7], g1[8], x0[8], x0[9])
-    run(g1[9], s0[0], g1[10])
+    run(g1[9])
+    gathered = len(sent)
+    run(s0[0], g1[10])
     run(x1[0], s0[1], s0[2], x1[1], s0[3], s0[4], x1[2], x1[3], s0[5], s0[6])
     run(x1[4], x1[5], s0[7], x1[6], x1[7], x1[8], x1[9])
-    run(s1[0], s0[8], s0[9])
-    run(*s1[1:])
+    run(s1[0])
+    flush(gathered)
+    run(s0[8], s0[9])
+    begun = len(sent)
+    run(*s1[1:10])
+    flush(begun)
+    run(s1[10])
+    crossed = len(sent)
+    run(*s1[11:])
+    flush(crossed)
 
     rzr[0] = rzs[0, 0]
     rzor[0] = rzos[0]
@@ -562,6 +581,7 @@
     take0 = pick0[:, 0:48].astype(BF16)
     take1 = pick1[:, 0:48].astype(BF16)
     behind = [lax.rem(z - e + 4, 4) for e in range(4)]
+    written = []
     for n in range(4):
         at = lanes(n, 768)
         rows = jnp.concatenate(
@@ -574,11 +594,15 @@
         second = jnp.dot(take1, rows, preferred_element_type=F32)
         layer = hb[:, at].astype(F32) + w0 * first + w1 * second
         for r in range(4):
-            out[r, :, at] = layer[4 * r:4 * r + 4].astype(out.dtype)
+            ob[r, :, at] = layer[4 * r:4 * r + 4].astype(BF16)
+        copy = pltpu.make_async_copy(ob.at[:, :, at], out.at[:, :, at], lsem.at[n])
+        copy.start()
+        written.append(copy)
 
     assert counter[0] <= NSEM
-    for copy in sent:
-        copy.wait_send()
+    flush(len(sent))
+    for copy in written:
+        copy.wait()
 
 
 def shards(
@@ -594,9 +618,9 @@
         kernel,
         out_shape=jax.ShapeDtypeStruct((4, 4, HALF), BF16),
         in_specs=[smem, hbm, hbm, hbm, hbm, hbm, hbm, vmem, vmem, vmem, hbm, hbm, hbm],
-        out_specs=vmem,
+        out_specs=pl.BlockSpec(memory_space=pltpu.HBM),
         scratch_shapes=[
-            V((4, 4, HALF), BF16), V((4, 128, 512), BF16), V((4, 128, 512), BF16),
+            V((4, 4, HALF), BF16), V((4, 4, HALF), BF16), V((4, 128, 512), BF16), V((4, 128, 512), BF16),
             V((4, 4, 512), BF16), V((4, 4, 512), BF16), V((4, 4, HALF), BF16),
             V((16, HALF), BF16), V((16, HALF), BF16), V((16, 128), F32), V((16, 128), F32),
             V((4, 8, HALF), BF16), V((4, 8, HALF), BF16), V((4, 1, HALF), F32), V((4, 1, HALF), F32),

time: 80 us -> 79.4 us (level)
  no operation moved by 1% of the time
where the time goes in v3:
time: 79.4 us; the launch traced here: 79.1 us
  Pallas kernels  77.6 us (98%)
  local copies, waits for them, and re-layouts  1.57 us (2%)
    pallas_call x1, Pallas kernels, shards(): pl.pallas_call(kernel, out_shape=jax.ShapeDtypeStruct((4, 4, HALF), BF16)...  77.6 us

profile of v3, /device:TPU:32, one launch (start us, length us, event | category | flops | bytes accessed | tf_op | source)
XLA Modules:
  0.0 79.1 jit_solution(3945517104788180852)
XLA Ops:
  0.0 77.6 %layer.1 = bf16[4,4,3072]{2,1,0:T(4,128)(2,1)} custom-call(s32[4]{0:T(128)} %lens.1, bf16[4,4,6144]{2,1,0:T(4,128)(2,1)} %q_hbm.1, bf16[4,128,1024]{2,1,0:T(8,128)(2,1)} %k_hbm.1, bf16[4,128,1024]{2,1,0:T(8,128)(2,1)} %v_hbm.1, bf16[4,4,1024]{2,1,0:T(4,128)(2,1)} %nk_hbm.1, bf16[4,4,1024]{2,1,0:T(4,128)(2,1)} %nv_hbm.1, bf16[4,4,6144]{2,1,0:T(4,128)(2,1)} %res_hbm.1, ...), custom_call_target="tpu_custom_call" | custom-call | tf_op jit(solution)/shard_map/layer/pallas_call | solution.py:617
  77.6 1.6 %copy.15 = bf16[4,4,3072]{2,1,0:T(4,128)(2,1)} copy(bf16[4,4,3072]{2,1,0:T(4,128)(2,1)} %layer.1) | data formatting | bytes 196608

commit v4 on v3

--- a/solution.py
+++ b/solution.py
@@ -550,9 +550,8 @@
 
     run(*g0[:4])
     second_wave()
-    run(*g0[4:6])
     run(g1[0])
-    run(*g0[6:])
+    run(*g0[4:])
     for copy in local[6:]:
         copy.wait()
     run(g1[1], x0[0], g1[2], g1[3], x0[1], g1[4], g1[5], x0[2], x0[3], g1[6])

time: 79.4 us -> 79.1 us (level)
  no operation moved by 1% of the time
where the time goes in v4:
time: 79.1 us; the launch traced here: 78.9 us
  Pallas kernels  77.3 us (98%)
  local copies, waits for them, and re-layouts  1.57 us (2%)
    pallas_call x1, Pallas kernels, shards(): pl.pallas_call(kernel, out_shape=jax.ShapeDtypeStruct((4, 4, HALF), BF16)...  77.3 us

profile of v4, /device:TPU:32, one launch (start us, length us, event | category | flops | bytes accessed | tf_op | source)
XLA Modules:
  0.0 78.9 jit_solution(7643932648540498647)
XLA Ops:
  0.0 77.3 %layer.1 = bf16[4,4,3072]{2,1,0:T(4,128)(2,1)} custom-call(s32[4]{0:T(128)} %lens.1, bf16[4,4,6144]{2,1,0:T(4,128)(2,1)} %q_hbm.1, bf16[4,128,1024]{2,1,0:T(8,128)(2,1)} %k_hbm.1, bf16[4,128,1024]{2,1,0:T(8,128)(2,1)} %v_hbm.1, bf16[4,4,1024]{2,1,0:T(4,128)(2,1)} %nk_hbm.1, bf16[4,4,1024]{2,1,0:T(4,128)(2,1)} %nv_hbm.1, bf16[4,4,6144]{2,1,0:T(4,128)(2,1)} %res_hbm.1, ...), custom_call_target="tpu_custom_call" | custom-call | tf_op jit(solution)/shard_map/layer/pallas_call | solution.py:616
  77.3 1.6 %copy.15 = bf16[4,4,3072]{2,1,0:T(4,128)(2,1)} copy(bf16[4,4,3072]{2,1,0:T(4,128)(2,1)} %layer.1) | data formatting | bytes 196608
